TPU v7x, 256 devices: a whole 4x4x8 slice. The times are simulated.
256 devices in a mesh: req: 4 (over x), exp: 64 (over z, y, core).
Axes of the slice: x: 4, y: 4, z: 8, core: 2. Of those that a mesh axis runs over, the one named last changes fastest.
Arguments:
- hidden: bfloat16 [256, 32, 2048], P(('req', 'exp')), may hold values from -6 to 6
- queries: bfloat16 [256, 32, 3072], P(('req', 'exp'))
- new_latent: bfloat16 [256, 32, 576], P(('req', 'exp')), may hold values from -6 to 6
- pages: bfloat16 [2048, 128, 576], P(('req', 'exp'))
- page_table: int32 [256, 8], P(('req', 'exp')), may hold values from 0 to 7, each once within a row
- cache_len: int32 [256], P(('req', 'exp')), may hold values from 1 to 992, as said below
- parents: int32 [256, 32], P(('req', 'exp')), may hold values from 0 to 30, as said below
- accept_path: int32 [256, 32], P(('req', 'exp')), may hold values from 0 to 31, as said below
- accept_count: int32 [256], P(('req', 'exp')), may hold values from 1 to 32, as said below
- key_up: bfloat16 [16, 128, 512], replicated, may hold values from -0.5 to 0.5
- value_up: bfloat16 [16, 512, 128], replicated, may hold values from -0.25 to 0.25
- out_proj: bfloat16 [2048, 2048], P(None, 'req'), may hold values from -0.125 to 0.125
- norm_gain: bfloat16 [2048], replicated, may hold values from 0.5 to 1.5
- route_ids: int32 [4, 64, 32, 6], P(None, 'exp'), may hold values from 0 to 63, all different within a row; in each aligned block of 32 rows (0 to 31, 32 to 63, ..., all dimensions but the last counted through in order) at most 6 rows name the same one
- route_weights: float32 [4, 64, 32, 6], P(None, 'exp'), may hold values from 0.2 to 1.2
- w_gate: bfloat16 [64, 2048, 1408], P('exp', None, 'req'), may hold values from -0.125 to 0.125
- w_up: bfloat16 [64, 2048, 1408], P('exp', None, 'req'), may hold values from -0.125 to 0.125
- w_down: bfloat16 [64, 1408, 2048], P('exp', 'req'), may hold values from -0.15625 to 0.15625
Outputs:
- layer_out: bfloat16 [256, 32, 2048], P(('req', 'exp'))
- new_pages: bfloat16 [2048, 128, 576], P(('req', 'exp'))
Inputs may be any that keep to these rules, and one draw needn't show every extreme that they name: `route_ids`: in each request no expert is named by more than 6 tokens, a bound that some block reaches. `page_table`: each row is an order of the 8 pages of the request's pool. `cache_len`: some request holds the largest length. parents[q, 0] = 0; for t >= 1 the parent of t is below t; one request's tree is a single chain. `accept_path`: entry k for k < accept_count is the ancestor at depth k of the last accepted token, entry 0 the root; later entries are 0. `accept_count`: one more than the depth of the last accepted token.
All inputs are finite; a program needn't handle non-finite values.
Results may differ from a plain program's by a relative error of at most 0.023.
Values may be sent and summed in bfloat16 or wider, within the bound.
A program may use at most 128 MiB of HBM per device.

v0:
```python
import math
import jax
import jax.numpy as jnp
from jax import lax
from jax.sharding import PartitionSpec as P

TOP = 6
TREE = 32


def ancestry(parent_row):
    count = parent_row.shape[0]
    ident = jnp.eye(count, dtype=jnp.int32)
    linked = (parent_row[:, None] == jnp.arange(count, dtype=jnp.int32)[None, :]).astype(jnp.int32)
    reach = jnp.minimum(ident + linked, 1)
    for sweep in range(count.bit_length()):
        reach = jnp.minimum(jnp.dot(reach, reach), 1)
    return reach


def attend(query_row, page_pool, table_row, length, parent_row, fresh, key_up, value_up):
    count = query_row.shape[0]
    heads = key_up.shape[0]
    nope = key_up.shape[1]
    latent = key_up.shape[2]
    shaped = query_row.reshape(count, heads, -1)
    scale = 1.0 / math.sqrt(shaped.shape[2])
    q_nope = shaped[:, :, :nope]
    q_rope = shaped[:, :, nope:]
    q_latent = jnp.einsum(
        "thn,hnc->thc", q_nope, key_up, preferred_element_type=jnp.float32
    ).astype(jnp.bfloat16)
    q_full = jnp.concatenate([q_latent, q_rope], axis=2)
    cache_rows = jnp.take(page_pool, table_row, axis=0).reshape(-1, page_pool.shape[2])
    score_cache = (
        jnp.einsum("thc,kc->thk", q_full, cache_rows, preferred_element_type=jnp.float32) * scale
    )
    score_tree = (
        jnp.einsum("thc,jc->thj", q_full, fresh, preferred_element_type=jnp.float32) * scale
    )
    live = jnp.arange(cache_rows.shape[0], dtype=jnp.int32) < length
    score_cache = jnp.where(live[None, None, :], score_cache, -1e30)
    score_tree = jnp.where(ancestry(parent_row)[:, None, :] > 0, score_tree, -1e30)
    peak = jnp.maximum(jnp.max(score_cache, axis=2), jnp.max(score_tree, axis=2))[:, :, None]
    exp_cache = jnp.exp(score_cache - peak)
    exp_tree = jnp.exp(score_tree - peak)
    total = jnp.sum(exp_cache, axis=2, keepdims=True) + jnp.sum(exp_tree, axis=2, keepdims=True)
    prob_cache = (exp_cache / total).astype(jnp.bfloat16)
    prob_tree = (exp_tree / total).astype(jnp.bfloat16)
    context = jnp.einsum(
        "thk,kc->thc", prob_cache, cache_rows[:, :latent], preferred_element_type=jnp.float32
    )
    context = context + jnp.einsum(
        "thj,jc->thc", prob_tree, fresh[:, :latent], preferred_element_type=jnp.float32
    )
    context = context.astype(jnp.bfloat16)
    head_out = jnp.einsum(
        "thc,hcv->thv", context, value_up, preferred_element_type=jnp.float32
    ).astype(jnp.bfloat16)
    return head_out.reshape(count, -1)


def write_rows(page_pool, table_row, length, path_row, count, fresh):
    pool_len = page_pool.shape[0]
    page_size = page_pool.shape[1]
    pool_ids = jnp.arange(pool_len, dtype=jnp.int32)
    match = table_row[None, :] == pool_ids[:, None]
    logical = jnp.sum(jnp.where(match, pool_ids[None, :], 0), axis=1)
    position = logical[:, None] * page_size + jnp.arange(page_size, dtype=jnp.int32)[None, :]
    offset = position - length
    valid = (offset >= 0) & (offset < count)
    source = jnp.take(path_row, jnp.clip(offset, 0, path_row.shape[0] - 1))
    written = jnp.take(fresh, source, axis=0)
    return jnp.where(valid[:, :, None], written, page_pool)


def slot_tables(route_rows, weight_rows, experts, capacity):
    expert_ids = jnp.arange(experts, dtype=jnp.int32)
    hits = route_rows[:, :, :, None] == expert_ids
    chosen = jnp.sum(hits.astype(jnp.int32), axis=2)
    weight_by = jnp.sum(jnp.where(hits, weight_rows[:, :, :, None], 0.0), axis=2)
    before = jnp.cumsum(chosen, axis=1) - chosen
    chosen_t = jnp.transpose(chosen, (0, 2, 1))
    before_t = jnp.transpose(before, (0, 2, 1))
    weight_t = jnp.transpose(weight_by, (0, 2, 1))
    slot_ids = jnp.arange(capacity, dtype=jnp.int32)
    placed = (chosen_t[:, :, None, :] > 0) & (
        before_t[:, :, None, :] == slot_ids[None, None, :, None]
    )
    weighted = jnp.where(placed, weight_t[:, :, None, :], 0.0)
    return (placed.astype(jnp.bfloat16), weighted)


def local(
    hidden,
    queries,
    new_latent,
    pages,
    page_table,
    cache_len,
    parents,
    accept_path,
    accept_count,
    key_up,
    value_up,
    out_proj,
    norm_gain,
    route_ids,
    route_weights,
    w_gate,
    w_up,
    w_down,
):
    width = hidden.shape[2]
    head_out = attend(
        queries[0], pages, page_table[0], cache_len[0], parents[0], new_latent[0], key_up, value_up
    )
    column_block = jnp.dot(
        lax.all_gather(head_out, "req", axis=0, tiled=True),
        out_proj,
        preferred_element_type=jnp.float32,
    ).astype(jnp.bfloat16)
    projected = lax.all_to_all(column_block, "req", split_axis=0, concat_axis=1, tiled=True)
    mixed = (hidden[0].astype(jnp.float32) + projected.astype(jnp.float32)).astype(jnp.bfloat16)
    mixed_f = mixed.astype(jnp.float32)
    normed = (
        mixed_f
        * lax.rsqrt(jnp.mean(mixed_f * mixed_f, axis=1, keepdims=True) + 1e-06)
        * norm_gain.astype(jnp.float32)
    ).astype(jnp.bfloat16)
    experts = lax.axis_size("exp") * w_gate.shape[0]
    capacity = max(2, min(TREE, 2 * TREE * TOP // experts))
    gate_local = w_gate[0]
    up_local = w_up[0]
    down_local = w_down[0]
    copies = lax.all_gather(normed[None], "req", axis=0, tiled=True)
    placed, weighted = slot_tables(route_ids[:, 0], route_weights[:, 0], experts, capacity)
    outbound = jnp.einsum(
        "gxct,gtd->xgcd", placed, copies, preferred_element_type=jnp.float32
    ).astype(jnp.bfloat16)
    slot_block = lax.all_to_all(outbound, "exp", split_axis=0, concat_axis=0, tiled=True)
    flat = slot_block.reshape(-1, width)
    gate_val = jnp.dot(flat, gate_local, preferred_element_type=jnp.float32)
    up_val = jnp.dot(flat, up_local, preferred_element_type=jnp.float32)
    active = (jax.nn.silu(gate_val) * up_val).astype(jnp.bfloat16)
    returned = lax.all_to_all(
        jnp.dot(active, down_local, preferred_element_type=jnp.float32)
        .astype(jnp.bfloat16)
        .reshape(slot_block.shape),
        "exp",
        split_axis=0,
        concat_axis=0,
        tiled=True,
    )
    partial_value = jnp.einsum("gxct,xgcd->gtd", weighted, returned.astype(jnp.float32))
    moe = lax.psum_scatter(
        partial_value.astype(jnp.bfloat16), "req", scatter_dimension=0, tiled=True
    ).astype(jnp.float32)[0]
    layer_out = (mixed_f + moe).astype(jnp.bfloat16)[None]
    new_pool = write_rows(
        pages, page_table[0], cache_len[0], accept_path[0], accept_count[0], new_latent[0]
    )
    return (layer_out, new_pool)


def solution(mesh):
    in_specs = (
        P(("req", "exp"), None, None),
        P(("req", "exp"), None, None),
        P(("req", "exp"), None, None),
        P(("req", "exp"), None, None),
        P(("req", "exp"), None),
        P(("req", "exp")),
        P(("req", "exp"), None),
        P(("req", "exp"), None),
        P(("req", "exp")),
        P(),
        P(),
        P(None, "req"),
        P(),
        P(None, "exp", None, None),
        P(None, "exp", None, None),
        P("exp", None, "req"),
        P("exp", None, "req"),
        P("exp", "req", None),
    )
    out_specs = (P(("req", "exp"), None, None), P(("req", "exp"), None, None))
    return jax.shard_map(local, mesh=mesh, in_specs=in_specs, out_specs=out_specs, check_vma=False)
```

profile of v0, /device:TPU:8, one launch (start us, length us, event | category | flops | bytes accessed | tf_op | source)
XLA Modules:
  0.0 495.9 jit_solution(1943214140383278034)
XLA Ops:
  7.2 0.0 copy-start
  7.2 1.4 reshape_squeeze.3
  8.6 0.7 slice.22
  9.3 0.7 fusion.78
  10.0 0.7 compare_and_fusion.1
  11.4 1.7 gather_fusion
  13.1 2.4 copy.166
  15.5 0.1 broadcast_bitcast_fusion
  15.6 0.4 fusion.18
  16.0 0.8 copy-done.6
  16.8 0.1 pad_maximum_fusion
  16.9 0.3 bitcast_select_fusion
  17.3 2.4 fusion.9
  19.7 0.1 copy.144
  19.7 0.4 convolution_minimum_fusion.4
  20.2 0.3 convolution_minimum_fusion.2
  20.5 0.3 fusion.23
  20.9 0.1 copy.143
  21.0 0.7 fusion.85
  21.7 0.1 copy.145
  21.8 2.1 fusion.10
  24.0 0.1 copy.146
  24.0 0.1 fusion.40
  24.1 0.1 copy.147
  24.2 2.1 divide_convert_fusion
  26.3 1.8 fusion.24
  28.1 2.5 fusion.22
  30.6 13.1 %all_gather.6 = bf16[128,2048]{1,0:T(8,128)(2,1)S(1)} all-gather(bf16[32,2048]{1,0:T(8,128)(2,1)S(1)} %bitcast.125), channel_id=1, replica_groups=mesh['req'=4,'exp'=64] {'req'}, dimensions={0}, use_global_device_ids=true | all-gather | bytes 655360 | tf_op jit(solution)/shard_map/all_gather | solution.py:119
  43.8 2.7 convolution_convert_fusion.2
  46.5 4.4 all-to-all-start
  50.9 0.2 convert_reduce_fusion
  51.1 0.1 reduce_window_sum.11
  51.2 5.6 %all-to-all-done = bf16[4,32,512]{2,1,0:T(8,128)(2,1)S(1)} async-done(((bf16[4,32,512]{2,1,0:T(8,128)(2,1)}), bf16[4,32,512]{2,1,0:T(8,128)(2,1)S(1)}, u32[]{:S(2)}, u32[]{:S(2)}) %all-to-all-start) | async-done | bytes 131104 | tf_op jit(solution)/shard_map/all_to_all | solution.py:123
  56.9 0.2 copy.151
  57.1 0.2 reshape.259
  57.4 0.1 multiply_reduce_fusion
  57.5 0.1 fusion.38
  57.6 13.7 %all_gather.7 = bf16[4,32,2048]{2,1,0:T(8,128)(2,1)S(1)} all-gather(bf16[1,32,2048]{2,1,0:T(8,128)(2,1)S(1)} %fusion.38), channel_id=1, replica_groups=mesh['req'=4,'exp'=64] {'req'}, dimensions={0}, use_global_device_ids=true | all-gather | bytes 655360 | tf_op jit(solution)/shard_map/all_gather | solution.py:136
  71.3 4.5 convert_bitcast_fusion
  75.8 10.3 %copy.157 = bf16[64,4,6,2048]{3,1,2,0:T(4,128)(2,1)} copy(bf16[64,4,6,2048]{3,0,2,1:T(8,128)(2,1)} %convert_bitcast_fusion) | data formatting | bytes 12582912 | tf_op jit(solution)/shard_map/convert_element_type | solution.py:140
  86.1 153.4 %all_to_all.23 = bf16[64,4,6,2048]{3,1,2,0:T(4,128)(2,1)S(1)} all-to-all(bf16[64,4,6,2048]{3,1,2,0:T(4,128)(2,1)} %copy.157), channel_id=1, replica_groups=mesh['req'=4,'exp'=64] {'exp'}, dimensions={0} | all-to-all | bytes 12582912 | tf_op jit(solution)/shard_map/all_to_all | solution.py:141
  239.5 10.7 %copy.158 = bf16[64,4,6,2048]{3,2,1,0:T(8,128)(2,1)} copy(bf16[64,4,6,2048]{3,1,2,0:T(4,128)(2,1)S(1)} %all_to_all.23) | data formatting | bytes 12582912 | tf_op jit(solution)/shard_map/all_to_all | solution.py:141
  250.2 11.1 %reshape.257 = bf16[1536,2048]{1,0:T(8,128)(2,1)} reshape(bf16[64,4,6,2048]{3,2,1,0:T(8,128)(2,1)} %copy.158) | data formatting | bytes 12582912 | tf_op jit(solution)/shard_map/reshape | solution.py:142
  261.3 7.0 %fusion.13 = f32[1536,352]{0,1:T(8,128)} fusion(bf16[1536,2048]{1,0:T(8,128)(2,1)} %reshape.257, bf16[1,2048,352]{1,2,0:T(8,128)(2,1)} %param.33), kind=kOutput, calls=%fused_computation.18 | convolution fusion | flops 2214592512 | bytes 9895936 | tf_op jit(solution)/shard_map/dot_general | solution.py:143
  268.3 12.2 %convolution_convert_fusion = bf16[1536,2048]{1,0:T(8,128)(2,1)} fusion(bf16[1,352,2048]{2,1,0:T(8,128)(2,1)} %param.35, bf16[1536,2048]{1,0:T(8,128)(2,1)} %reshape.257, f32[1536,352]{0,1:T(8,128)} %fusion.13, bf16[1,2048,352]{1,2,0:T(8,128)(2,1)} %param.34), kind=kOutput, calls=%fused_computation.3 | convolution fusion | flops 4435574784 | bytes 17629184 | tf_op jit(solution)/shard_map/dot_general | solution.py:147
  280.4 11.4 %reshape.258 = bf16[64,4,6,2048]{3,2,1,0:T(8,128)(2,1)} reshape(bf16[1536,2048]{1,0:T(8,128)(2,1)} %convolution_convert_fusion) | data formatting | bytes 12582912 | tf_op jit(solution)/shard_map/reshape | solution.py:149
  291.8 18.8 %copy.159 = bf16[64,4,6,2048]{3,1,2,0:T(4,128)(2,1)} copy(bf16[64,4,6,2048]{3,2,1,0:T(8,128)(2,1)} %reshape.258) | data formatting | bytes 12582912 | tf_op jit(solution)/shard_map/reshape | solution.py:149
  310.7 5.7 %all-to-all-start.2 = ((bf16[64,4,6,2048]{3,1,2,0:T(4,128)(2,1)}), bf16[64,4,6,2048]{3,1,2,0:T(4,128)(2,1)}, u32[]{:S(2)}, u32[]{:S(2)}) async-start(bf16[64,4,6,2048]{3,1,2,0:T(4,128)(2,1)} %copy.159), calls=%async_computation.2 | async-start | bytes 12582912 | tf_op jit(solution)/shard_map/all_to_all | solution.py:146
  316.4 0.0 reduce-scatter.2.cloned.1.call-start
  316.5 0.1 select_reduce_fusion.1
  316.6 0.3 select_reduce_fusion
  316.9 140.8 %all-to-all-done.2 = bf16[64,4,6,2048]{3,1,2,0:T(4,128)(2,1)} async-done(((bf16[64,4,6,2048]{3,1,2,0:T(4,128)(2,1)}), bf16[64,4,6,2048]{3,1,2,0:T(4,128)(2,1)}, u32[]{:S(2)}, u32[]{:S(2)}) %all-to-all-start.2) | async-done | bytes 6291488 | tf_op jit(solution)/shard_map/all_to_all | solution.py:146
  457.7 10.5 %fusion.6 = bf16[4,32,2048]{2,1,0:T(8,128)(2,1)} fusion(bf16[64,4,6,2048]{3,1,2,0:T(4,128)(2,1)} %all-to-all-done.2, bf16[4,64,32]{1,2,0:T(8,128)(2,1)S(1)} %bitcast.128, s32[4,64,32]{1,2,0:T(8,128)S(1)} %subtract_bitcast_fusion, pred[4,64,32]{1,2,0:T(8,128)(4,1)S(1)} %compare_bitcast_fusion), kind=kOutput, calls=%fused_computation.10 | convolution fusion | flops 201474048 | bytes 6873088 | tf_op jit(solution)/shard_map/gxct,xgcd->gtd/dot_general | solution.py:155
  468.2 0.0 reduce-scatter.2.cloned.1.call-update
  468.2 0.1 bitcast_clamp_fusion
  468.3 0.5 copy-done.2
  468.8 6.6 %gather_fusion.1 = s32[1024]{0:T(1024)S(1)} fusion(s32[32]{0:T(128)S(1)} %bitcast.120, s32[1024]{0:T(1024)S(1)} %bitcast_clamp_fusion), kind=kCustom, calls=%fused_computation.1 | custom fusion | bytes 12288 | tf_op jit(solution)/shard_map/jit(_take)/gather | solution.py:72
  475.4 0.1 fusion.68
  475.5 4.0 gather_fusion.2
  479.5 1.4 copy.161
  481.6 0.1 fusion.77
  481.7 2.6 select_select_fusion
  484.3 2.9 reduce-scatter.2.cloned.1.call-done
  487.2 1.7 fusion.39
  (49 shorter events, 0.3 us)
Async XLA Ops:
  7.2 8.4 %copy-start = (bf16[16,128,512]{2,1,0:T(8,128)(2,1)S(1)}, bf16[16,128,512]{2,1,0:T(8,128)(2,1)}, u32[]{:S(2)}) copy-start(bf16[16,128,512]{2,1,0:T(8,128)(2,1)} %param.27) | copy-start | bytes 6291460
  7.2 4.2 copy-start.4
  11.3 4.7 copy-start.9
  11.4 4.2 copy-start.11
  15.5 1.4 copy-start.5
  16.0 0.8 copy-start.6
  17.2 2.5 copy-start.15
  17.2 3.7 copy-start.3
  17.2 3.7 copy-start.7
  17.2 3.7 copy-start.10
  30.6 20.3 %copy-start.12 = (s32[4,1,32,6]{2,1,3,0:T(1,128)S(1)}, s32[4,1,32,6]{2,1,3,0:T(1,128)}, u32[]{:S(2)}) copy-start(s32[4,1,32,6]{2,1,3,0:T(1,128)} %param.31) | copy-start | bytes 9220
  30.6 20.6 %copy-start.14 = (bf16[2048]{0:T(1024)(128)(2,1)S(1)}, bf16[2048]{0:T(1024)(128)(2,1)}, u32[]{:S(2)}) copy-start(bf16[2048]{0:T(1024)(128)(2,1)} %param.30) | copy-start | bytes 12292
  46.5 10.9 %copy-start.8 = (bf16[1,32,2048]{2,1,0:T(8,128)(2,1)S(1)}, bf16[1,32,2048]{2,1,0:T(8,128)(2,1)}, u32[]{:S(2)}) copy-start(bf16[1,32,2048]{2,1,0:T(8,128)(2,1)} %param.18) | copy-start | bytes 393220
  46.5 10.4 %all-to-all-start = ((bf16[4,32,512]{2,1,0:T(8,128)(2,1)}), bf16[4,32,512]{2,1,0:T(8,128)(2,1)S(1)}, u32[]{:S(2)}, u32[]{:S(2)}) async-start(bf16[4,32,512]{2,1,0:T(8,128)(2,1)} %bitcast.14), calls=%async_computation | async-start | bytes 262144 | tf_op jit(solution)/shard_map/all_to_all | solution.py:123
  310.7 5.8 %copy-start.13 = (f32[4,1,32,6]{2,1,3,0:T(1,128)S(1)}, f32[4,1,32,6]{2,1,3,0:T(1,128)}, u32[]{:S(2)}) copy-start(f32[4,1,32,6]{2,1,3,0:T(1,128)} %param.32) | copy-start | bytes 9220
  310.7 5.8 %copy-start.16 = (s32[1,8]{1,0:T(1,128)S(1)}, s32[1,8]{1,0:T(1,128)}, u32[]{:S(2)}) copy-start(s32[1,8]{1,0:T(1,128)} %param.22) | copy-start | bytes 100
  310.7 147.0 %all-to-all-start.2 = ((bf16[64,4,6,2048]{3,1,2,0:T(4,128)(2,1)}), bf16[64,4,6,2048]{3,1,2,0:T(4,128)(2,1)}, u32[]{:S(2)}, u32[]{:S(2)}) async-start(bf16[64,4,6,2048]{3,1,2,0:T(4,128)(2,1)} %copy.159), calls=%async_computation.2 | async-start | bytes 12582912 | tf_op jit(solution)/shard_map/all_to_all | solution.py:146
  316.4 170.8 %reduce-scatter.2.cloned.1.call-start = ((), (), s32[]{:S(2)}) async-start(), calls=%async_computation.4 | async-start | bytes 655360 | tf_op jit(solution)/shard_map/reduce_scatter | solution.py:156
  468.2 0.7 copy-start.2
  481.7 7.2 %copy-start.1 = (bf16[16,128,512]{2,1,0:T(8,128)(2,1)S(1)}, bf16[16,128,512]{2,1,0:T(8,128)(2,1)}, u32[]{:S(2)}) copy-start(bf16[16,128,512]{2,1,0:T(8,128)(2,1)} %param.27) | copy-start | bytes 6291460
Sparse Core Ops, SparseCore 0:
  468.3 18.8 reduce-scatter.1
where the time goes:
time: 503 us; the launch traced here: 496 us
  blocking collectives  180 us (36%)
  waiting for transfers between devices  149 us (30%)
  local copies, waits for them, and re-layouts  82.8 us (16%)
  matrix products  45.8 us (9%)
  between operations  16 us (3%)
  other arithmetic  11.5 us (2%)
  starting transfers between devices  10.2 us (2%)
    all_to_all x1, blocking collectives, local(): lax.all_to_all(outbound, 'exp', split_axis=0, concat_axis=0, tiled=True)  153 us
    all_to_all x1, waiting for transfers between devices, local(): lax.all_to_all(jnp.dot(active, down_local, preferred_element_type=jnp.flo...  141 us
    reshape x2, local copies, waits for them, and re-layouts, local(): returned = lax.all_to_all(jnp.dot(active, down_local, preferred_element_t...  30.2 us
    all_gather x1, blocking collectives, local(): copies = lax.all_gather(normed[None], 'req', axis=0, tiled=True)  13.7 us
    all_gather x1, blocking collectives, local(): lax.all_gather(head_out, 'req', axis=0, tiled=True)  13.1 us
    dot_general x1, matrix products, local(): jnp.dot(active, down_local, preferred_element_type=jnp.float32)  12.2 us
    reshape x1, local copies, waits for them, and re-layouts, local(): flat = slot_block.reshape(-1, width)  11.1 us
    all_to_all x1, local copies, waits for them, and re-layouts, local(): lax.all_to_all(outbound, 'exp', split_axis=0, concat_axis=0, tiled=True)  10.7 us
  transfers between devices with their start and end apart: 3, of which 3 were waited for; matrix products, arithmetic and copies ran while one was open for 3% of the time, Pallas kernels for 0%

commit v1 on v0

--- a/solution.py
+++ b/solution.py
@@ -133,7 +133,12 @@
     gate_local = w_gate[0]
     up_local = w_up[0]
     down_local = w_down[0]
-    copies = lax.all_gather(normed[None], "req", axis=0, tiled=True)
+    ring = [normed[None]]
+    for hop in range(3):
+        ring.append(lax.ppermute(ring[-1], "req", [(dev, (dev + 1) % 4) for dev in range(4)]))
+    copies = jnp.roll(
+        jnp.concatenate(ring[::-1], axis=0), (lax.axis_index("req") + 1) * ring[0].shape[0], axis=0
+    )
     placed, weighted = slot_tables(route_ids[:, 0], route_weights[:, 0], experts, capacity)
     outbound = jnp.einsum(
         "gxct,gtd->xgcd", placed, copies, preferred_element_type=jnp.float32

time: 503 us -> 521 us (1.036)
  waiting for transfers between devices: 149 us -> 176 us
  blocking collectives: 180 us -> 167 us
    ppermute x0 -> x3, waiting for transfers between devices: none -> 19.6 us  [local(): lax.ppermute(ring[-1], 'req', [(dev, (dev + 1) % 4) for dev in range(4)])]
    all_gather x1 -> x0, blocking collectives: 13.7 us -> none  [local(): copies = lax.all_gather(normed[None], 'req', axis=0, tiled=True)]
    reduce_scatter x1, waiting for transfers between devices: 2.91 us -> 9.24 us  [local(): lax.psum_scatter(partial_value.astype(jnp.bfloat16), 'req', scatter_dimen...]
  transfers between devices with their start and end apart: 3 -> 6, of which waited for: 3 -> 6; matrix products, arithmetic and copies ran while one was open for 3% -> 2% of each run, Pallas kernels for 0% -> 0%
where the time goes in v1:
time: 521 us; the launch traced here: 512 us
  waiting for transfers between devices  176 us (34%)
  blocking collectives  167 us (32%)
  local copies, waits for them, and re-layouts  81.7 us (16%)
  matrix products  45.5 us (9%)
  between operations  16 us (3%)
  other arithmetic  15.5 us (3%)
  starting transfers between devices  11 us (2%)
    all_to_all x1, blocking collectives, local(): lax.all_to_all(outbound, 'exp', split_axis=0, concat_axis=0, tiled=True)  153 us
    all_to_all x1, waiting for transfers between devices, local(): lax.all_to_all(jnp.dot(active, down_local, preferred_element_type=jnp.flo...  141 us
    reshape x2, local copies, waits for them, and re-layouts, local(): returned = lax.all_to_all(jnp.dot(active, down_local, preferred_element_t...  30.2 us
    ppermute x3, waiting for transfers between devices, local(): lax.ppermute(ring[-1], 'req', [(dev, (dev + 1) % 4) for dev in range(4)])  19.6 us
    all_gather x1, blocking collectives, local(): lax.all_gather(head_out, 'req', axis=0, tiled=True)  13.1 us
    dot_general x1, matrix products, local(): jnp.dot(active, down_local, preferred_element_type=jnp.float32)  12.2 us
    reshape x1, local copies, waits for them, and re-layouts, local(): flat = slot_block.reshape(-1, width)  11.1 us
    all_to_all x1, local copies, waits for them, and re-layouts, local(): lax.all_to_all(outbound, 'exp', split_axis=0, concat_axis=0, tiled=True)  10.7 us
  transfers between devices with their start and end apart: 6, of which 6 were waited for; matrix products, arithmetic and copies ran while one was open for 2% of the time, Pallas kernels for 0%

profile of v1, /device:TPU:8, one launch (start us, length us, event | category | flops | bytes accessed | tf_op | source)
XLA Modules:
  0.0 512.1 jit_solution(15684940632295591858)
XLA Ops:
  7.2 1.3 fusion.79
  8.5 1.2 compare_and_fusion.1
  9.7 1.2 reshape_squeeze.3
  11.7 0.8 select_reduce_fusion.1
  12.4 0.1 bitcast_clamp_fusion
  12.5 6.6 %gather_fusion.1 = s32[1024]{0:T(1024)S(1)} fusion(s32[32]{0:T(128)S(1)} %bitcast.120, s32[1024]{0:T(1024)S(1)} %bitcast_clamp_fusion), kind=kCustom, calls=%fused_computation.1 | custom fusion | bytes 12288 | tf_op jit(solution)/shard_map/jit(_take)/gather | solution.py:72
  19.1 0.7 fusion.69
  19.9 1.7 gather_fusion
  21.6 2.4 copy.166
  24.1 0.1 broadcast_bitcast_fusion
  24.2 1.6 bitcast_select_fusion
  25.8 0.4 fusion.18
  26.3 0.8 copy-done.5
  27.1 0.1 pad_maximum_fusion
  27.2 2.4 fusion.9
  29.6 0.1 copy.144
  29.7 0.4 convolution_minimum_fusion.4
  30.1 0.3 convolution_minimum_fusion.2
  30.4 0.3 fusion.23
  30.8 0.1 copy.143
  30.9 0.7 fusion.87
  31.7 0.1 copy.145
  31.7 2.1 fusion.10
  33.9 0.1 copy.146
  33.9 0.1 fusion.41
  34.0 0.1 copy.147
  34.1 2.2 divide_convert_fusion
  36.4 1.8 fusion.24
  38.1 2.5 fusion.22
  40.7 13.1 %all_gather.3 = bf16[128,2048]{1,0:T(8,128)(2,1)S(1)} all-gather(bf16[32,2048]{1,0:T(8,128)(2,1)S(1)} %bitcast.125), channel_id=1, replica_groups=mesh['req'=4,'exp'=64] {'req'}, dimensions={0}, use_global_device_ids=true | all-gather | bytes 655360 | tf_op jit(solution)/shard_map/all_gather | solution.py:119
  53.8 2.7 convolution_convert_fusion.2
  56.6 4.4 all-to-all-start
  61.0 6.0 %all-to-all-done = bf16[4,32,512]{2,1,0:T(8,128)(2,1)S(1)} async-done(((bf16[4,32,512]{2,1,0:T(8,128)(2,1)}), bf16[4,32,512]{2,1,0:T(8,128)(2,1)S(1)}, u32[]{:S(2)}, u32[]{:S(2)}) %all-to-all-start) | async-done | bytes 131104 | tf_op jit(solution)/shard_map/all_to_all | solution.py:123
  67.0 0.2 copy.151
  67.2 0.2 reshape.259
  67.4 0.1 multiply_reduce_fusion
  67.6 0.1 fusion.39
  67.7 0.6 collective-permute-start
  68.4 0.2 convert_reduce_fusion
  68.5 0.1 reduce_window_sum.11
  68.6 6.6 %collective-permute-done = bf16[1,32,2048]{2,1,0:T(8,128)(2,1)S(1)} collective-permute-done((bf16[1,32,2048]{2,1,0:T(8,128)(2,1)S(1)}, bf16[1,32,2048]{2,1,0:T(8,128)(2,1)S(1)}, u32[]{:S(2)}, u32[]{:S(2)}) %collective-permute-start) | collective-permute-done | bytes 131104 | tf_op jit(solution)/shard_map/ppermute | solution.py:138
  75.3 6.9 %collective-permute-done.1 = bf16[1,32,2048]{2,1,0:T(8,128)(2,1)S(1)} collective-permute-done((bf16[1,32,2048]{2,1,0:T(8,128)(2,1)S(1)}, bf16[1,32,2048]{2,1,0:T(8,128)(2,1)S(1)}, u32[]{:S(2)}, u32[]{:S(2)}) %collective-permute-start.1) | collective-permute-done | bytes 131104 | tf_op jit(solution)/shard_map/ppermute | solution.py:138
  82.1 0.2 collective-permute-start.2
  82.3 6.1 %collective-permute-done.2 = bf16[1,32,2048]{2,1,0:T(8,128)(2,1)S(1)} collective-permute-done((bf16[1,32,2048]{2,1,0:T(8,128)(2,1)S(1)}, bf16[1,32,2048]{2,1,0:T(8,128)(2,1)S(1)}, u32[]{:S(2)}, u32[]{:S(2)}) %collective-permute-start.2) | collective-permute-done | bytes 131104 | tf_op jit(solution)/shard_map/ppermute | solution.py:138
  88.6 4.5 convert_bitcast_fusion
  93.1 10.3 %copy.157 = bf16[64,4,6,2048]{3,1,2,0:T(4,128)(2,1)} copy(bf16[64,4,6,2048]{3,0,2,1:T(8,128)(2,1)} %convert_bitcast_fusion) | data formatting | bytes 12582912 | tf_op jit(solution)/shard_map/convert_element_type | solution.py:145
  103.4 153.4 %all_to_all.23 = bf16[64,4,6,2048]{3,1,2,0:T(4,128)(2,1)S(1)} all-to-all(bf16[64,4,6,2048]{3,1,2,0:T(4,128)(2,1)} %copy.157), channel_id=1, replica_groups=mesh['req'=4,'exp'=64] {'exp'}, dimensions={0} | all-to-all | bytes 12582912 | tf_op jit(solution)/shard_map/all_to_all | solution.py:146
  256.8 10.7 %copy.158 = bf16[64,4,6,2048]{3,2,1,0:T(8,128)(2,1)} copy(bf16[64,4,6,2048]{3,1,2,0:T(4,128)(2,1)S(1)} %all_to_all.23) | data formatting | bytes 12582912 | tf_op jit(solution)/shard_map/all_to_all | solution.py:146
  267.6 11.1 %reshape.257 = bf16[1536,2048]{1,0:T(8,128)(2,1)} reshape(bf16[64,4,6,2048]{3,2,1,0:T(8,128)(2,1)} %copy.158) | data formatting | bytes 12582912 | tf_op jit(solution)/shard_map/reshape | solution.py:147
  278.7 6.6 %fusion.13 = f32[1536,352]{0,1:T(8,128)} fusion(bf16[1536,2048]{1,0:T(8,128)(2,1)} %reshape.257, bf16[1,2048,352]{1,2,0:T(8,128)(2,1)S(1)} %copy-done.16), kind=kOutput, calls=%fused_computation.18 | convolution fusion | flops 2214592512 | bytes 9895936 | tf_op jit(solution)/shard_map/dot_general | solution.py:148
  285.3 12.2 %convolution_convert_fusion = bf16[1536,2048]{1,0:T(8,128)(2,1)} fusion(bf16[1,352,2048]{2,1,0:T(8,128)(2,1)} %param.35, bf16[1536,2048]{1,0:T(8,128)(2,1)} %reshape.257, f32[1536,352]{0,1:T(8,128)} %fusion.13, bf16[1,2048,352]{1,2,0:T(8,128)(2,1)} %param.34), kind=kOutput, calls=%fused_computation.3 | convolution fusion | flops 4435574784 | bytes 17629184 | tf_op jit(solution)/shard_map/dot_general | solution.py:152
  297.5 11.4 %reshape.258 = bf16[64,4,6,2048]{3,2,1,0:T(8,128)(2,1)} reshape(bf16[1536,2048]{1,0:T(8,128)(2,1)} %convolution_convert_fusion) | data formatting | bytes 12582912 | tf_op jit(solution)/shard_map/reshape | solution.py:154
  308.9 18.8 %copy.159 = bf16[64,4,6,2048]{3,1,2,0:T(4,128)(2,1)} copy(bf16[64,4,6,2048]{3,2,1,0:T(8,128)(2,1)} %reshape.258) | data formatting | bytes 12582912 | tf_op jit(solution)/shard_map/reshape | solution.py:154
  327.7 5.8 %all-to-all-start.2 = ((bf16[64,4,6,2048]{3,1,2,0:T(4,128)(2,1)}), bf16[64,4,6,2048]{3,1,2,0:T(4,128)(2,1)}, u32[]{:S(2)}, u32[]{:S(2)}) async-start(bf16[64,4,6,2048]{3,1,2,0:T(4,128)(2,1)} %copy.159), calls=%async_computation.2 | async-start | bytes 12582912 | tf_op jit(solution)/shard_map/all_to_all | solution.py:151
  333.5 0.0 reduce-scatter.2.cloned.1.call-start
  333.6 0.3 select_reduce_fusion
  333.8 140.9 %all-to-all-done.2 = bf16[64,4,6,2048]{3,1,2,0:T(4,128)(2,1)} async-done(((bf16[64,4,6,2048]{3,1,2,0:T(4,128)(2,1)}), bf16[64,4,6,2048]{3,1,2,0:T(4,128)(2,1)}, u32[]{:S(2)}, u32[]{:S(2)}) %all-to-all-start.2) | async-done | bytes 6291488 | tf_op jit(solution)/shard_map/all_to_all | solution.py:151
  474.7 10.5 %fusion.6 = bf16[4,32,2048]{2,1,0:T(8,128)(2,1)} fusion(bf16[64,4,6,2048]{3,1,2,0:T(4,128)(2,1)} %all-to-all-done.2, bf16[4,64,32]{1,2,0:T(8,128)(2,1)S(1)} %bitcast.128, s32[4,64,32]{1,2,0:T(8,128)S(1)} %subtract_bitcast_fusion, pred[4,64,32]{1,2,0:T(8,128)(4,1)S(1)} %compare_bitcast_fusion), kind=kOutput, calls=%fused_computation.10 | convolution fusion | flops 201474048 | bytes 6873088 | tf_op jit(solution)/shard_map/gxct,xgcd->gtd/dot_general | solution.py:160
  485.3 4.0 gather_fusion.2
  489.3 1.4 copy.161
  491.4 0.1 fusion.78
  491.5 2.6 select_select_fusion
  494.1 9.2 %reduce-scatter.2.cloned.1.call-done = bf16[1,32,2048]{2,1,0:T(8,128)(2,1)} async-done(((bf16[4,32,2048]{2,1,0:T(8,128)(2,1)}), bf16[1,32,2048]{2,1,0:T(8,128)(2,1)}) %reduce-scatter.2.cloned.1.call-update) | async-done | bytes 131088 | tf_op jit(solution)/shard_map/reduce_scatter | solution.py:161
  503.4 1.7 fusion.40
  (67 shorter events, 0.4 us)
Async XLA Ops:
  7.2 18.6 %copy-start = (bf16[16,128,512]{2,1,0:T(8,128)(2,1)S(1)}, bf16[16,128,512]{2,1,0:T(8,128)(2,1)}, u32[]{:S(2)}) copy-start(bf16[16,128,512]{2,1,0:T(8,128)(2,1)} %param.27) | copy-start | bytes 6291460
  7.2 5.3 %copy-start.2 = (s32[1,32]{1,0:T(1,128)S(1)}, s32[1,32]{1,0:T(1,128)}, u32[]{:S(2)}) copy-start(s32[1,32]{1,0:T(1,128)} %param.25) | copy-start | bytes 388
  11.0 8.1 %copy-start.10 = (bf16[32,16,192]{2,1,0:T(8,128)(2,1)}, bf16[32,16,192]{2,1,0:T(8,128)(2,1)S(1)}, u32[]{:S(2)}) copy-start(bf16[32,16,192]{2,1,0:T(8,128)(2,1)S(1)} %reshape_squeeze.3) | copy-start | bytes 589828
  12.5 7.3 %copy-start.4 = (bf16[8,128,576]{1,2,0:T(8,128)(2,1)S(1)}, bf16[8,128,576]{1,2,0:T(8,128)(2,1)}, u32[]{:S(2)}) copy-start(bf16[8,128,576]{1,2,0:T(8,128)(2,1)} %param.21) | copy-start | bytes 3538948
  19.9 4.2 copy-start.18
  19.9 4.2 slice-start.1
  21.6 4.2 slice-start
  24.2 2.1 copy-start.11
  25.8 3.8 copy-start.7
  26.3 0.8 copy-start.5
  27.1 2.5 copy-start.17
  27.1 3.7 copy-start.3
  27.2 3.7 copy-start.6
  27.2 3.7 copy-start.12
  33.9 2.5 copy-start.8
  40.6 20.4 %copy-start.15 = (bf16[2048]{0:T(1024)(128)(2,1)S(1)}, bf16[2048]{0:T(1024)(128)(2,1)}, u32[]{:S(2)}) copy-start(bf16[2048]{0:T(1024)(128)(2,1)} %param.30) | copy-start | bytes 12292
  53.8 13.6 %copy-start.9 = (bf16[1,32,2048]{2,1,0:T(8,128)(2,1)S(1)}, bf16[1,32,2048]{2,1,0:T(8,128)(2,1)}, u32[]{:S(2)}) copy-start(bf16[1,32,2048]{2,1,0:T(8,128)(2,1)} %param.18) | copy-start | bytes 393220
  56.6 11.8 %copy-start.13 = (s32[4,1,32,6]{2,1,3,0:T(1,128)S(1)}, s32[4,1,32,6]{2,1,3,0:T(1,128)}, u32[]{:S(2)}) copy-start(s32[4,1,32,6]{2,1,3,0:T(1,128)} %param.31) | copy-start | bytes 9220
  56.6 10.4 %all-to-all-start = ((bf16[4,32,512]{2,1,0:T(8,128)(2,1)}), bf16[4,32,512]{2,1,0:T(8,128)(2,1)S(1)}, u32[]{:S(2)}, u32[]{:S(2)}) async-start(bf16[4,32,512]{2,1,0:T(8,128)(2,1)} %bitcast.14), calls=%async_computation | async-start | bytes 262144 | tf_op jit(solution)/shard_map/all_to_all | solution.py:123
  67.7 7.6 %collective-permute-start = (bf16[1,32,2048]{2,1,0:T(8,128)(2,1)S(1)}, bf16[1,32,2048]{2,1,0:T(8,128)(2,1)S(1)}, u32[]{:S(2)}, u32[]{:S(2)}) collective-permute-start(bf16[1,32,2048]{2,1,0:T(8,128)(2,1)S(1)} %fusion.39), channel_id=1, source_target_pairs={{0,64},{64,128},{128,192},{192,0},{1,65},{65,129},{129,193},{193,1... | collective-permute-start | bytes 393224 | tf_op jit(solution)/shard_map/ppermute | solution.py:138
  75.3 6.9 %collective-permute-start.1 = (bf16[1,32,2048]{2,1,0:T(8,128)(2,1)S(1)}, bf16[1,32,2048]{2,1,0:T(8,128)(2,1)S(1)}, u32[]{:S(2)}, u32[]{:S(2)}) collective-permute-start(bf16[1,32,2048]{2,1,0:T(8,128)(2,1)S(1)} %collective-permute-done), channel_id=1, source_target_pairs={{0,64},{64,128},{128,192},{192,0},{1,65},{65,129},{129,193},{193,1... | collective-permute-start | bytes 393224 | tf_op jit(solution)/shard_map/ppermute | solution.py:138
  82.1 6.3 %collective-permute-start.2 = (bf16[1,32,2048]{2,1,0:T(8,128)(2,1)S(1)}, bf16[1,32,2048]{2,1,0:T(8,128)(2,1)S(1)}, u32[]{:S(2)}, u32[]{:S(2)}) collective-permute-start(bf16[1,32,2048]{2,1,0:T(8,128)(2,1)S(1)} %collective-permute-done.1), channel_id=1, source_target_pairs={{0,64},{64,128},{128,192},{192,0},{1,65},{65,129},{129,193},{193,1... | collective-permute-start | bytes 393224 | tf_op jit(solution)/shard_map/ppermute | solution.py:138
  267.6 11.1 %copy-start.16 = (bf16[1,2048,352]{1,2,0:T(8,128)(2,1)S(1)}, bf16[1,2048,352]{1,2,0:T(8,128)(2,1)}, u32[]{:S(2)}) copy-start(bf16[1,2048,352]{1,2,0:T(8,128)(2,1)} %param.33) | copy-start | bytes 4325380
  327.7 5.8 %copy-start.14 = (f32[4,1,32,6]{2,1,3,0:T(1,128)S(1)}, f32[4,1,32,6]{2,1,3,0:T(1,128)}, u32[]{:S(2)}) copy-start(f32[4,1,32,6]{2,1,3,0:T(1,128)} %param.32) | copy-start | bytes 9220
  327.7 147.0 %all-to-all-start.2 = ((bf16[64,4,6,2048]{3,1,2,0:T(4,128)(2,1)}), bf16[64,4,6,2048]{3,1,2,0:T(4,128)(2,1)}, u32[]{:S(2)}, u32[]{:S(2)}) async-start(bf16[64,4,6,2048]{3,1,2,0:T(4,128)(2,1)} %copy.159), calls=%async_computation.2 | async-start | bytes 12582912 | tf_op jit(solution)/shard_map/all_to_all | solution.py:151
  333.5 169.9 %reduce-scatter.2.cloned.1.call-start = ((), (), s32[]{:S(2)}) async-start(), calls=%async_computation.4 | async-start | bytes 655360 | tf_op jit(solution)/shard_map/reduce_scatter | solution.py:161
  491.5 13.5 %copy-start.1 = (bf16[16,128,512]{2,1,0:T(8,128)(2,1)S(1)}, bf16[16,128,512]{2,1,0:T(8,128)(2,1)}, u32[]{:S(2)}) copy-start(bf16[16,128,512]{2,1,0:T(8,128)(2,1)} %param.27) | copy-start | bytes 6291460
Sparse Core Ops, SparseCore 0:
  485.4 17.9 reduce-scatter.1
